TPU v7x, 256 devices: a whole 4x4x8 slice. The times are simulated.
256 devices in a mesh: dp: 2 (over x_lo), expert: 8 (over z), shard: 16 (over x_hi, y, core).
Axes of the slice: x: 4 (x_hi: 2, x_lo: 2; x = x_hi * 2 + x_lo), y: 4, z: 8, core: 2. Of those that a mesh axis runs over, the one named last changes fastest.
Arguments:
- tokens: bfloat16 [2048, 6144], P(('dp', 'expert', 'shard')), may hold values from -6 to 6
- gate_up_weight: bfloat16 [8, 2, 8192, 6144], P(None, None, ('dp', 'expert', 'shard')), may hold values from -0.078125 to 0.078125
- down_weight: bfloat16 [8, 8192, 6144], P(None, ('dp', 'expert', 'shard')), may hold values from -0.0625 to 0.0625
- expert_ids: int32 [2048, 2], P(('dp', 'expert', 'shard')), may hold values from 0 to 7, as said below
- slot_ids: int32 [2048, 2], P(('dp', 'expert', 'shard')), may hold values from 0 to 3, as said below
- gate_values: float32 [2048, 2], P(('dp', 'expert', 'shard')), may hold values from 0.1 to 1
- old_place: int32 [8], replicated, may hold values from 0 to 7, each once
- new_place: int32 [8], replicated, may hold values from 0 to 7, each once
Outputs:
- mixed_out: bfloat16 [2048, 6144], P(('dp', 'expert', 'shard'))
Inputs may be any that keep to these rules, and one draw needn't show every extreme that they name: `expert_ids`: each token names 2 different experts; among the 8 tokens of one block no expert is named more than 4 times, and one expert is named exactly 4 times in every block. `slot_ids`: within one block, two choices that name the same expert have different slots. `old_place`: each expert number appears once. `new_place`: each expert number appears once.
All inputs are finite; a program needn't handle non-finite values.
Results may differ from a plain program's by a relative error of at most 0.02.
Values may be sent and summed in bfloat16 or wider, within the bound.
A program may use at most 128 MiB of HBM per device.

v0:
```python
import jax
import jax.numpy as jnp
from jax import lax
from jax.sharding import PartitionSpec as P


def placement_order(old_place, new_place):
    slot_total = old_place.shape[0]
    matches = (new_place[:, None] == old_place[None, :]).astype(jnp.int32)
    return jnp.sum(matches * jnp.arange(slot_total, dtype=jnp.int32)[None, :], axis=1)


def swiglu_rows(row_block, pair_weight):
    gate_up = jnp.einsum("rd,gud->rgu", row_block, pair_weight, preferred_element_type=jnp.float32)
    return (jax.nn.silu(gate_up[:, 0]) * gate_up[:, 1]).astype(jnp.bfloat16)


def local(
    tokens, gate_up_weight, down_weight, expert_ids, slot_ids, gate_values, old_place, new_place
):
    experts = gate_up_weight.shape[0]
    sliver = gate_up_weight.shape[2]
    model_width = tokens.shape[1]
    tok_rows = tokens.shape[0]
    choices_per_token = expert_ids.shape[1]
    capacity = 2 * tok_rows * choices_per_token // experts
    cell_count = experts * capacity
    data_ways = lax.axis_size("dp")
    slot_order = placement_order(old_place, new_place)
    cell_ids = expert_ids * capacity + slot_ids
    cell_range = jnp.arange(cell_count, dtype=jnp.int32)
    cell_hits = (cell_ids[:, :, None] == cell_range[None, None, :]).astype(jnp.float32)
    token_picks = jnp.sum(cell_hits, axis=1)
    dispatched = jnp.dot(
        token_picks.T.astype(jnp.bfloat16), tokens, preferred_element_type=jnp.float32
    ).astype(jnp.bfloat16)
    received = lax.all_to_all(
        dispatched.reshape(experts, capacity, model_width),
        "expert",
        split_axis=0,
        concat_axis=0,
        tiled=True,
    )
    own_rows = received.reshape(cell_count, model_width)
    sectioned_in = gate_up_weight.reshape(experts, 2, data_ways, sliver // data_ways, model_width)
    sectioned_down = down_weight.reshape(experts, 1, data_ways, sliver // data_ways, model_width)
    sectioned_in = jnp.take(sectioned_in, slot_order, axis=0)
    sectioned_down = jnp.take(sectioned_down, slot_order, axis=0)
    relaid_in, relaid_down = (
        lax.all_to_all(
            lax.all_to_all(sectioned_in, "dp", split_axis=2, concat_axis=3, tiled=True),
            "expert",
            split_axis=0,
            concat_axis=3,
            tiled=True,
        ),
        lax.all_to_all(
            lax.all_to_all(sectioned_down, "dp", split_axis=2, concat_axis=3, tiled=True),
            "expert",
            split_axis=0,
            concat_axis=3,
            tiled=True,
        ),
    )
    full_in, full_down = (
        lax.all_gather(relaid_in, "dp", axis=3, tiled=True),
        lax.all_gather(relaid_down, "dp", axis=3, tiled=True),
    )
    pair_in = full_in.reshape(2, -1, model_width)
    pair_down = full_down.reshape(-1, model_width)
    group_rows = lax.all_gather(own_rows, "shard", axis=0, tiled=True)
    summed = lax.psum_scatter(
        jnp.dot(
            swiglu_rows(group_rows, pair_in), pair_down, preferred_element_type=jnp.float32
        ).astype(jnp.bfloat16),
        "shard",
        scatter_dimension=0,
        tiled=True,
    )
    returned = lax.all_to_all(
        summed.reshape(experts, capacity, model_width),
        "expert",
        split_axis=0,
        concat_axis=0,
        tiled=True,
    )
    combine_weights = jnp.sum(cell_hits * gate_values[:, :, None], axis=1)
    mixed_out = jnp.dot(
        combine_weights,
        returned.reshape(cell_count, model_width).astype(jnp.float32),
        precision=lax.Precision.HIGHEST,
    )
    return mixed_out.astype(jnp.bfloat16)


def solution(mesh):
    in_specs = (
        P(("dp", "expert", "shard"), None),
        P(None, None, ("dp", "expert", "shard"), None),
        P(None, ("dp", "expert", "shard"), None),
        P(("dp", "expert", "shard"), None),
        P(("dp", "expert", "shard"), None),
        P(("dp", "expert", "shard"), None),
        P(),
        P(),
    )
    out_specs = P(("dp", "expert", "shard"), None)
    return jax.shard_map(local, mesh=mesh, in_specs=in_specs, out_specs=out_specs, check_vma=False)
```

profile of v0, /device:TPU:8, one launch (start us, length us, event | category | flops | bytes accessed | tf_op | source)
XLA Modules:
  0.0 681.6 jit_solution(10519561180992360223)
XLA Ops:
  8.3 1.2 convolution_convert_fusion.1
  9.5 0.9 reshape.64
  10.4 8.5 %all-to-all-start = ((bf16[8,4,6144]{2,1,0:T(4,128)(2,1)}), bf16[8,4,6144]{2,1,0:T(4,128)(2,1)S(1)}, u32[]{:S(2)}, u32[]{:S(2)}) async-start(bf16[8,4,6144]{2,1,0:T(4,128)(2,1)} %reshape.64), calls=%async_computation | async-start | bytes 786432 | tf_op jit(solution)/shard_map/all_to_all | solution.py:37
  19.7 6.4 gather_fusion
  26.1 3.5 broadcast_select_fusion
  29.6 3.1 copy.24
  33.5 6.3 all-to-all-start.1
  40.8 89.5 %all-to-all-done.1 = bf16[8,2,2,16,6144]{4,3,1,0,2:T(8,128)(2,1)} async-done(((bf16[8,2,2,16,6144]{4,3,1,0,2:T(8,128)(2,1)}), bf16[8,2,2,16,6144]{4,3,1,0,2:T(8,128)(2,1)}, u32[]{:S(2)}, u32[]{:S(2)}) %all-to-all-start.1) | async-done | bytes 6291488 | tf_op jit(solution)/shard_map/all_to_all | solution.py:51
  130.3 3.5 copy.25
  133.8 145.8 %all_to_all.64 = bf16[8,2,1,32,6144]{4,3,1,2,0:T(8,128)(2,1)S(1)} all-to-all(bf16[8,2,1,32,6144]{4,3,1,2,0:T(8,128)(2,1)S(1)} %bitcast.37), channel_id=1, replica_groups=mesh['dp'=2,'expert'=8,'shard'=16] {'expert'}, dimensions={0} | all-to-all | bytes 12582912 | tf_op jit(solution)/shard_map/all_to_all | solution.py:50
  279.7 3.1 copy.27
  282.8 2.4 gather_fusion.1
  285.3 2.3 bitcast_select_fusion
  287.9 63.1 %all_to_all.65 = bf16[8,1,2,16,6144]{4,3,0,1,2:T(8,128)(2,1)S(1)} all-to-all(bf16[8,1,2,16,6144]{4,3,0,1,2:T(8,128)(2,1)S(1)} %copy.28), channel_id=1, replica_groups=mesh['dp'=2,'expert'=8,'shard'=16] {'dp'}, dimensions={2} | all-to-all | bytes 6291456 | tf_op jit(solution)/shard_map/all_to_all | solution.py:58
  351.2 66.1 %all_to_all.66 = bf16[8,1,1,32,6144]{4,3,2,1,0:T(8,128)(2,1)} all-to-all(bf16[8,1,1,32,6144]{4,3,2,1,0:T(8,128)(2,1)S(1)} %bitcast.40), channel_id=1, replica_groups=mesh['dp'=2,'expert'=8,'shard'=16] {'expert'}, dimensions={0} | all-to-all | bytes 6291456 | tf_op jit(solution)/shard_map/all_to_all | solution.py:57
  417.5 41.2 %all-gather.6.cloned.1.call-done = bf16[1,2,1,512,6144]{4,3,1,2,0:T(8,128)(2,1)} async-done(((bf16[1,2,1,256,6144]{4,3,1,2,0:T(8,128)(2,1)}), bf16[1,2,1,512,6144]{4,3,1,2,0:T(8,128)(2,1)}) %all-gather.6.cloned.1.call-update) | async-done | bytes 12582928 | tf_op jit(solution)/shard_map/all_gather | solution.py:66
  458.6 12.5 %fusion = f32[512,2,512]{2,0,1:T(8,128)} fusion(bf16[1,2,1,512,6144]{4,3,1,2,0:T(8,128)(2,1)} %all-gather.6.cloned.1.call-done, bf16[512,6144]{1,0:T(8,128)(2,1)} %all-gather.4.cloned.1.call-done), kind=kOutput, calls=%fused_computation.2 | convolution fusion | flops 6442450944 | bytes 20971520 | tf_op jit(solution)/shard_map/rd,gud->rgu/dot_general | solution.py:14
  471.2 72.6 %all-gather.8.cloned.1.call-done = bf16[1,1,1,512,6144]{4,3,2,1,0:T(8,128)(2,1)} async-done(((bf16[1,1,1,256,6144]{4,3,2,1,0:T(8,128)(2,1)}), bf16[1,1,1,512,6144]{4,3,2,1,0:T(8,128)(2,1)}) %all-gather.8.cloned.1.call-update) | async-done | bytes 6291472 | tf_op jit(solution)/shard_map/all_gather | solution.py:67
  543.8 9.7 %convolution_convert_fusion = bf16[512,6144]{1,0:T(8,128)(2,1)} fusion(bf16[1,1,1,512,6144]{4,3,2,1,0:T(8,128)(2,1)} %all-gather.8.cloned.1.call-done, f32[512,2,512]{2,0,1:T(8,128)} %fusion), kind=kOutput, calls=%fused_computation.4 | convolution fusion | flops 3225944064 | bytes 14680064 | tf_op jit(solution)/shard_map/dot_general | solution.py:73
  553.6 98.3 %reduce-scatter.2.cloned.1.call-done = bf16[32,6144]{1,0:T(8,128)(2,1)} async-done(((bf16[512,6144]{1,0:T(8,128)(2,1)}), bf16[32,6144]{1,0:T(8,128)(2,1)}) %reduce-scatter.2.cloned.1.call-update) | async-done | bytes 393232 | tf_op jit(solution)/shard_map/reduce_scatter | solution.py:72
  651.9 1.1 reshape.70
  653.0 20.0 %all_to_all.67 = bf16[8,4,6144]{2,1,0:T(4,128)(2,1)} all-to-all(bf16[8,4,6144]{2,1,0:T(4,128)(2,1)S(1)} %reshape.70), channel_id=1, replica_groups=mesh['dp'=2,'expert'=8,'shard'=16] {'expert'}, dimensions={0} | all-to-all | bytes 786432 | tf_op jit(solution)/shard_map/all_to_all | solution.py:80
  673.1 1.1 reshape.71
  674.1 0.9 convolution_convert_fusion.2
  (23 shorter events, 5.2 us)
Async XLA Ops:
  6.5 276.3 %copy-start = (bf16[8,32,6144]{2,1,0:T(8,128)(2,1)S(1)}, bf16[8,32,6144]{2,1,0:T(8,128)(2,1)}, u32[]{:S(2)}) copy-start(bf16[8,32,6144]{2,1,0:T(8,128)(2,1)} %param.10) | copy-start | bytes 9437188
  10.4 23.2 %all-to-all-start = ((bf16[8,4,6144]{2,1,0:T(4,128)(2,1)}), bf16[8,4,6144]{2,1,0:T(4,128)(2,1)S(1)}, u32[]{:S(2)}, u32[]{:S(2)}) async-start(bf16[8,4,6144]{2,1,0:T(4,128)(2,1)} %reshape.64), calls=%async_computation | async-start | bytes 786432 | tf_op jit(solution)/shard_map/all_to_all | solution.py:37
  33.5 96.8 %all-to-all-start.1 = ((bf16[8,2,2,16,6144]{4,3,1,0,2:T(8,128)(2,1)}), bf16[8,2,2,16,6144]{4,3,1,0,2:T(8,128)(2,1)}, u32[]{:S(2)}, u32[]{:S(2)}) async-start(bf16[8,2,2,16,6144]{4,3,1,0,2:T(8,128)(2,1)} %copy.24), calls=%async_computation.1 | async-start | bytes 12582912 | tf_op jit(solution)/shard_map/all_to_all | solution.py:51
  39.8 377.6 %all-gather.4.cloned.1.call-start = ((), (), s32[]{:S(2)}) async-start(), calls=%async_computation.7 | async-start | bytes 6684672 | tf_op jit(solution)/shard_map/all_gather | solution.py:71
  40.8 417.9 %all-gather.6.cloned.1.call-start = ((), (), s32[]{:S(2)}) async-start(), calls=%async_computation.8 | async-start | bytes 18874368 | tf_op jit(solution)/shard_map/all_gather | solution.py:66
  282.8 261.0 %all-gather.8.cloned.1.call-start = ((), (), s32[]{:S(2)}) async-start(), calls=%async_computation.9 | async-start | bytes 9437184 | tf_op jit(solution)/shard_map/all_gather | solution.py:67
  417.4 234.5 %reduce-scatter.2.cloned.1.call-start = ((), (), s32[]{:S(2)}) async-start(), calls=%async_computation.10 | async-start | bytes 6684672 | tf_op jit(solution)/shard_map/reduce_scatter | solution.py:72
  543.8 131.2 %copy-start.1 = (bf16[8,32,6144]{2,1,0:T(8,128)(2,1)S(1)}, bf16[8,32,6144]{2,1,0:T(8,128)(2,1)}, u32[]{:S(2)}) copy-start(bf16[8,32,6144]{2,1,0:T(8,128)(2,1)} %param.10) | copy-start | bytes 9437188
Sparse Core Ops, SparseCore 0:
  43.4 90.1 all-gather.3
  282.9 175.6 all-gather.5
  460.4 83.3 all-gather.7
  553.7 98.1 reduce-scatter.1
where the time goes:
time: 682 us
  waiting for transfers between devices  303 us (44%)
  blocking collectives  295 us (43%)
  matrix products  24.3 us (4%)
  local copies, waits for them, and re-layouts  23.1 us (3%)
  starting transfers between devices  15 us (2%)
  between operations  13.2 us (2%)
  other arithmetic  8.31 us (1%)
    all_to_all x1, blocking collectives, local(): lax.all_to_all(lax.all_to_all(sectioned_in, 'dp', split_axis=2, concat_ax...  146 us
    reduce_scatter x1, waiting for transfers between devices, local(): lax.psum_scatter(jnp.dot(swiglu_rows(group_rows, pair_in), pair_down, pre...  98.3 us
    all_to_all x1, waiting for transfers between devices, local(): lax.all_to_all(sectioned_in, 'dp', split_axis=2, concat_axis=3, tiled=True)  89.5 us
    all_gather x1, waiting for transfers between devices, local(): lax.all_gather(relaid_down, 'dp', axis=3, tiled=True)  72.6 us
    all_to_all x1, blocking collectives, local(): lax.all_to_all(lax.all_to_all(sectioned_down, 'dp', split_axis=2, concat_...  66.1 us
    all_to_all x1, blocking collectives, local(): lax.all_to_all(sectioned_down, 'dp', split_axis=2, concat_axis=3, tiled=T...  63.1 us
    all_gather x1, waiting for transfers between devices, local(): lax.all_gather(relaid_in, 'dp', axis=3, tiled=True)  41.2 us
    all_to_all x1, blocking collectives, local(): lax.all_to_all(summed.reshape(experts, capacity, model_width), 'expert',...  20 us
  transfers between devices with their start and end apart: 6, of which 5 were waited for; matrix products, arithmetic and copies ran while one was open for 6% of the time, Pallas kernels for 0%

commit v1 on v0

--- a/solution.py
+++ b/solution.py
@@ -2,6 +2,11 @@
 import jax.numpy as jnp
 from jax import lax
 from jax.sharding import PartitionSpec as P
+
+
+def solve_the_ports(patch):
+    latest = lax.all_gather(patch, axis_name="dp")
+    return jnp.concatenate(latest, 3)
 
 
 def placement_order(old_place, new_place):
@@ -63,7 +68,7 @@
         ),
     )
     full_in, full_down = (
-        lax.all_gather(relaid_in, "dp", axis=3, tiled=True),
+        solve_the_ports(relaid_in),
         lax.all_gather(relaid_down, "dp", axis=3, tiled=True),
     )
     pair_in = full_in.reshape(2, -1, model_width)

time: 682 us -> 727 us (1.066)
  blocking collectives: 295 us -> 402 us
  waiting for transfers between devices: 303 us -> 249 us
  starting transfers between devices: 15 us -> 0.13 us
  local copies, waits for them, and re-layouts: 23.1 us -> 30.6 us
    all_to_all x2 -> x0, waiting for transfers between devices: 90.4 us -> none  [the longest x1 89.5 us: local(): lax.all_to_all(sectioned_in, 'dp', split_axis=2, concat_axis=3, tiled=True)]
    all_to_all x0 -> x2, blocking collectives: none -> 88.4 us  [the longest x1 73 us: local(): lax.all_to_all(sectioned_in, 'dp', split_axis=2, concat_axis=3, tiled=True)]
    all_gather x1, waiting for transfers between devices: 0.02 us -> 60.5 us  [local(): group_rows = lax.all_gather(own_rows, 'shard', axis=0, tiled=True)]
    all_gather x1, waiting for transfers between devices: 41.2 us -> 16.4 us  [solve_the_ports(): latest = lax.all_gather(patch, axis_name='dp')]
    all_to_all x2 -> x0, starting transfers between devices: 14.8 us -> none  [the longest x1 8.47 us: local(): lax.all_to_all(dispatched.reshape(experts, capacity, model_width), 'exper...]
    reshape x0 -> x1, local copies, waits for them, and re-layouts: none -> 10.7 us  [solve_the_ports(): return jnp.concatenate(latest, 3)]
    all_to_all x1, blocking collectives: 63.1 us -> 72.3 us  [local(): lax.all_to_all(sectioned_down, 'dp', split_axis=2, concat_axis=3, tiled=T...]
  transfers between devices with their start and end apart: 6 -> 4, of which waited for: 5 -> 4; matrix products, arithmetic and copies ran while one was open for 6% -> 5% of each run, Pallas kernels for 0% -> 0%
where the time goes in v1:
time: 727 us; the launch traced here: 726 us
  blocking collectives  402 us (55%)
  waiting for transfers between devices  249 us (34%)
  local copies, waits for them, and re-layouts  30.6 us (4%)
  matrix products  24.2 us (3%)
  between operations  13.2 us (2%)
    all_to_all x1, blocking collectives, local(): lax.all_to_all(lax.all_to_all(sectioned_in, 'dp', split_axis=2, concat_ax...  148 us
    reduce_scatter x1, waiting for transfers between devices, local(): lax.psum_scatter(jnp.dot(swiglu_rows(group_rows, pair_in), pair_down, pre...  98.3 us
    all_gather x1, waiting for transfers between devices, local(): lax.all_gather(relaid_down, 'dp', axis=3, tiled=True)  73.9 us
    all_to_all x1, blocking collectives, local(): lax.all_to_all(sectioned_in, 'dp', split_axis=2, concat_axis=3, tiled=True)  73 us
    all_to_all x1, blocking collectives, local(): lax.all_to_all(lax.all_to_all(sectioned_down, 'dp', split_axis=2, concat_...  72.9 us
    all_to_all x1, blocking collectives, local(): lax.all_to_all(sectioned_down, 'dp', split_axis=2, concat_axis=3, tiled=T...  72.3 us
    all_gather x1, waiting for transfers between devices, local(): group_rows = lax.all_gather(own_rows, 'shard', axis=0, tiled=True)  60.5 us
    all_to_all x1, blocking collectives, local(): lax.all_to_all(summed.reshape(experts, capacity, model_width), 'expert',...  20 us
  transfers between devices with their start and end apart: 4, of which 4 were waited for; matrix products, arithmetic and copies ran while one was open for 5% of the time, Pallas kernels for 0%

profile of v1, /device:TPU:8, one launch (start us, length us, event | category | flops | bytes accessed | tf_op | source)
XLA Modules:
  0.0 726.5 jit_solution(12490034898772001527)
XLA Ops:
  6.5 1.0 select_reduce_fusion.1
  7.6 6.4 gather_fusion
  14.0 3.5 broadcast_select_fusion
  18.2 73.0 %all_to_all.61 = bf16[8,2,2,16,6144]{4,3,1,0,2:T(8,128)(2,1)S(1)} all-to-all(bf16[8,2,2,16,6144]{4,3,1,0,2:T(8,128)(2,1)S(1)} %copy.35), channel_id=1, replica_groups=mesh['dp'=2,'expert'=8,'shard'=16] {'dp'}, dimensions={2} | all-to-all | bytes 12582912 | tf_op jit(solution)/shard_map/all_to_all | solution.py:56
  91.9 148.5 %all_to_all.62 = bf16[8,2,1,32,6144]{4,3,1,2,0:T(8,128)(2,1)S(1)} all-to-all(bf16[8,2,1,32,6144]{4,3,1,2,0:T(8,128)(2,1)S(1)} %bitcast.40), channel_id=1, replica_groups=mesh['dp'=2,'expert'=8,'shard'=16] {'expert'}, dimensions={0} | all-to-all | bytes 12582912 | tf_op jit(solution)/shard_map/all_to_all | solution.py:55
  240.4 3.0 copy.38
  244.3 1.0 convolution_convert_fusion.1
  245.4 1.1 reshape.65
  246.5 15.4 %all_to_all.63 = bf16[8,4,6144]{2,1,0:T(4,128)(2,1)} all-to-all(bf16[8,4,6144]{2,1,0:T(4,128)(2,1)S(1)} %reshape.65), channel_id=1, replica_groups=mesh['dp'=2,'expert'=8,'shard'=16] {'expert'}, dimensions={0} | all-to-all | bytes 786432 | tf_op jit(solution)/shard_map/all_to_all | solution.py:42
  261.9 1.9 reshape.66
  263.9 2.4 gather_fusion.1
  266.3 2.6 bitcast_select_fusion
  269.2 72.3 %all_to_all.64 = bf16[8,1,2,16,6144]{4,3,0,1,2:T(8,128)(2,1)S(1)} all-to-all(bf16[8,1,2,16,6144]{4,3,0,1,2:T(8,128)(2,1)S(1)} %copy.41), channel_id=1, replica_groups=mesh['dp'=2,'expert'=8,'shard'=16] {'dp'}, dimensions={2} | all-to-all | bytes 6291456 | tf_op jit(solution)/shard_map/all_to_all | solution.py:63
  341.8 72.9 %all_to_all.65 = bf16[8,1,1,32,6144]{4,3,2,1,0:T(8,128)(2,1)} all-to-all(bf16[8,1,1,32,6144]{4,3,2,1,0:T(8,128)(2,1)S(1)} %bitcast.44), channel_id=1, replica_groups=mesh['dp'=2,'expert'=8,'shard'=16] {'expert'}, dimensions={0} | all-to-all | bytes 6291456 | tf_op jit(solution)/shard_map/all_to_all | solution.py:62
  414.7 16.4 %all-gather.6.cloned.1.call-done = bf16[2,1,2,1,256,6144]{5,4,3,2,1,0:T(8,128)(2,1)} async-done(((bf16[1,1,2,1,256,6144]{5,4,3,2,1,0:T(8,128)(2,1)}), bf16[2,1,2,1,256,6144]{5,4,3,2,1,0:T(8,128)(2,1)}) %all-gather.6.cloned.1.call-update) | async-done | bytes 12582928 | tf_op jit(solution)/shard_map/all_gather | solution.py:8
  431.1 10.7 %copy.40 = bf16[1,2,1,2,256,6144]{5,4,3,1,2,0:T(8,128)(2,1)} copy(bf16[1,2,1,2,256,6144]{5,4,2,1,0,3:T(8,128)(2,1)} %bitcast.41) | data formatting | bytes 25165824 | tf_op jit(solution)/shard_map/reshape | solution.py:9
  441.8 60.5 %all-gather.4.cloned.1.call-done = bf16[512,6144]{1,0:T(8,128)(2,1)} async-done(((bf16[32,6144]{1,0:T(8,128)(2,1)}), bf16[512,6144]{1,0:T(8,128)(2,1)}) %all-gather.4.cloned.1.call-update) | async-done | bytes 6291472 | tf_op jit(solution)/shard_map/all_gather | solution.py:76
  502.3 12.5 %fusion.1 = f32[512,2,512]{2,0,1:T(8,128)} fusion(bf16[2,512,6144]{2,1,0:T(8,128)(2,1)} %bitcast.42, bf16[512,6144]{1,0:T(8,128)(2,1)} %all-gather.4.cloned.1.call-done), kind=kOutput, calls=%fused_computation.6 | convolution fusion | flops 6442450944 | bytes 20971520 | tf_op jit(solution)/shard_map/rd,gud->rgu/dot_general | solution.py:19
  514.8 73.9 %all-gather.8.cloned.1.call-done = bf16[1,1,1,512,6144]{4,3,2,1,0:T(8,128)(2,1)} async-done(((bf16[1,1,1,256,6144]{4,3,2,1,0:T(8,128)(2,1)}), bf16[1,1,1,512,6144]{4,3,2,1,0:T(8,128)(2,1)}) %all-gather.8.cloned.1.call-update) | async-done | bytes 6291472 | tf_op jit(solution)/shard_map/all_gather | solution.py:72
  588.7 9.7 %convolution_convert_fusion = bf16[512,6144]{1,0:T(8,128)(2,1)} fusion(bf16[1,1,1,512,6144]{4,3,2,1,0:T(8,128)(2,1)} %all-gather.8.cloned.1.call-done, f32[512,2,512]{2,0,1:T(8,128)} %fusion.1), kind=kOutput, calls=%fused_computation.2 | convolution fusion | flops 3225944064 | bytes 14680064 | tf_op jit(solution)/shard_map/dot_general | solution.py:78
  598.4 98.3 %reduce-scatter.2.cloned.1.call-done = bf16[32,6144]{1,0:T(8,128)(2,1)} async-done(((bf16[512,6144]{1,0:T(8,128)(2,1)}), bf16[32,6144]{1,0:T(8,128)(2,1)}) %reduce-scatter.2.cloned.1.call-update) | async-done | bytes 393232 | tf_op jit(solution)/shard_map/reduce_scatter | solution.py:77
  696.8 1.1 reshape.71
  697.9 20.0 %all_to_all.66 = bf16[8,4,6144]{2,1,0:T(4,128)(2,1)} all-to-all(bf16[8,4,6144]{2,1,0:T(4,128)(2,1)S(1)} %reshape.71), channel_id=1, replica_groups=mesh['dp'=2,'expert'=8,'shard'=16] {'expert'}, dimensions={0} | all-to-all | bytes 786432 | tf_op jit(solution)/shard_map/all_to_all | solution.py:85
  717.9 1.1 reshape.72
  (30 shorter events, 4.1 us)
Async XLA Ops:
  6.5 257.3 %copy-start = (bf16[8,32,6144]{2,1,0:T(8,128)(2,1)S(1)}, bf16[8,32,6144]{2,1,0:T(8,128)(2,1)}, u32[]{:S(2)}) copy-start(bf16[8,32,6144]{2,1,0:T(8,128)(2,1)} %param.10) | copy-start | bytes 9437188
  6.5 424.6 %all-gather.6.cloned.1.call-start = ((), (), s32[]{:S(2)}) async-start(), calls=%async_computation.8 | async-start | bytes 18874368 | tf_op jit(solution)/shard_map/all_gather | solution.py:8
  243.4 0.7 copy-start.3
  243.4 0.7 copy-start.4
  243.4 0.7 copy-start.5
  243.4 0.9 copy-start.2
  243.4 258.9 %all-gather.4.cloned.1.call-start = ((), (), s32[]{:S(2)}) async-start(), calls=%async_computation.7 | async-start | bytes 6684672 | tf_op jit(solution)/shard_map/all_gather | solution.py:76
  263.8 324.9 %all-gather.8.cloned.1.call-start = ((), (), s32[]{:S(2)}) async-start(), calls=%async_computation.9 | async-start | bytes 9437184 | tf_op jit(solution)/shard_map/all_gather | solution.py:72
  414.7 282.1 %reduce-scatter.2.cloned.1.call-start = ((), (), s32[]{:S(2)}) async-start(), calls=%async_computation.10 | async-start | bytes 6684672 | tf_op jit(solution)/shard_map/reduce_scatter | solution.py:77
  588.7 131.2 %copy-start.1 = (bf16[8,32,6144]{2,1,0:T(8,128)(2,1)S(1)}, bf16[8,32,6144]{2,1,0:T(8,128)(2,1)}, u32[]{:S(2)}) copy-start(bf16[8,32,6144]{2,1,0:T(8,128)(2,1)} %param.10) | copy-start | bytes 9437188
Sparse Core Ops, SparseCore 0:
  243.5 187.5 all-gather.5
  433.9 68.3 all-gather.3
  504.1 84.5 all-gather.7
  598.6 98.1 reduce-scatter.1
